TPU v7x, 256 devices: a whole 4x4x8 slice. The times are simulated.
256 devices in a mesh: row: 16 (over z, y_hi), col: 16 (over x, y_lo, core).
Axes of the slice: x: 4, y: 4 (y_hi: 2, y_lo: 2; y = y_hi * 2 + y_lo), z: 8, core: 2. Of those that a mesh axis runs over, the one named last changes fastest.
Arguments:
- tokens: bfloat16 [1024, 14336], P('col', 'row'), may hold values from -6 to 6
- gate_weight: bfloat16 [14336, 26624], P('row', 'col'), may hold values from -0.046875 to 0.046875
- up_weight: bfloat16 [14336, 26624], P('row', 'col'), may hold values from -0.046875 to 0.046875
- upstream: bfloat16 [1024, 26624], P('row', 'col'), may hold values from -0.1875 to 0.1875
Outputs:
- grad_gate: bfloat16 [14336, 26624], P('row', 'col')
- grad_up: bfloat16 [14336, 26624], P('row', 'col')
All inputs are finite; a program needn't handle non-finite values.
Results may differ from a plain program's by a relative error of at most 0.005.
Values may be sent and summed in bfloat16 or wider, within the bound.
A program may use at most 128 MiB of HBM per device.

v0:
```python
import jax
import jax.numpy as jnp
from jax import lax
from jax.sharding import PartitionSpec as P


def swiglu_grads(preacts, cotangent_rows, hidden_cols):
    gate_pre = preacts[:, :hidden_cols]
    up_pre = preacts[:, hidden_cols:]
    squash = jax.nn.sigmoid(gate_pre)
    cotangent = cotangent_rows.astype(jnp.float32)
    d_up = cotangent * gate_pre * squash
    d_gate = cotangent * up_pre * squash * (1.0 + gate_pre * (1.0 - squash))
    return jnp.concatenate([d_gate, d_up], axis=1).astype(jnp.bfloat16)


def local(tokens, gate_weight, up_weight, upstream):
    hidden_cols = gate_weight.shape[1]
    numbers = (((0,), (0,)), ((), ()))
    weights = jnp.concatenate([gate_weight, up_weight], axis=1)
    gathered = lax.all_gather(tokens, "col", axis=0, tiled=True)
    partial_pre = jnp.dot(gathered, weights, preferred_element_type=jnp.float32)
    preacts = lax.psum(partial_pre, "row")
    cotangent_all = lax.all_gather(upstream, "row", axis=0, tiled=True)
    gradients = swiglu_grads(preacts, cotangent_all, hidden_cols)
    weight_grads = lax.dot_general(gathered, gradients, numbers, preferred_element_type=jnp.float32)
    rounded = weight_grads.astype(jnp.bfloat16)
    return (rounded[:, :hidden_cols], rounded[:, hidden_cols:])


def solution(mesh):
    return jax.shard_map(
        local,
        mesh=mesh,
        in_specs=(P("col", "row"), P("row", "col"), P("row", "col"), P("row", "col")),
        out_specs=(P("row", "col"), P("row", "col")),
        check_vma=False,
    )
```

profile of v0, /device:TPU:2, one launch (start us, length us, event | category | flops | bytes accessed | tf_op | source)
XLA Modules:
  0.0 761.3 jit_solution(7752807111683964820)
XLA Ops:
  7.2 0.0 all-gather.5.cloned.1.call-start
  7.2 0.7 all-gather.5.cloned.1.call-update
  7.9 0.0 all-gather.3.cloned.1.call-start
  7.9 0.7 all-gather.3.cloned.1.call-update
  8.6 0.0 all-reduce.2.cloned.1.call-start
  8.7 39.8 %all-gather.5.cloned.1.call-done = bf16[1024,896]{1,0:T(8,128)(2,1)} async-done(((bf16[64,896]{1,0:T(8,128)(2,1)}), bf16[1024,896]{1,0:T(8,128)(2,1)}) %all-gather.5.cloned.1.call-update) | async-done | bytes 1835024 | tf_op jit(solution)/shard_map/all_gather | solution.py:21
  48.5 13.5 %convolution_bitcast_fusion = f32[1024,3328]{0,1:T(8,128)} fusion(bf16[1024,896]{1,0:T(8,128)(2,1)} %all-gather.5.cloned.1.call-done, bf16[896,1664]{1,0:T(8,128)(2,1)} %param.6, bf16[896,1664]{1,0:T(8,128)(2,1)} %param.5), kind=kOutput, calls=%fused_computation | convolution fusion | flops 6118834176 | bytes 21430272 | tf_op jit(solution)/shard_map/dot_general | solution.py:22
  62.0 0.0 all-reduce.2.cloned.1.call-update
  62.0 83.9 %all-gather.3.cloned.1.call-done = bf16[1024,1664]{1,0:T(8,128)(2,1)} async-done(((bf16[64,1664]{1,0:T(8,128)(2,1)}), bf16[1024,1664]{1,0:T(8,128)(2,1)}) %all-gather.3.cloned.1.call-update) | async-done | bytes 3407888 | tf_op jit(solution)/shard_map/all_gather | solution.py:24
  145.9 4.2 copy.9
  150.2 576.0 %all-reduce.2.cloned.1.call-done = f32[1024,3328]{0,1:T(8,128)} async-done(((f32[1024,3328]{0,1:T(8,128)}), f32[1024,3328]{0,1:T(8,128)}) %all-reduce.2.cloned.1.call-update) | async-done | bytes 13631504 | tf_op jit(solution)/shard_map/psum | solution.py:23
  726.2 0.0 copy-start
  726.2 6.7 fusion.2
  732.9 0.0 copy-done
  732.9 10.8 %fusion.8 = bf16[896,3328]{0,1:T(8,128)(2,1)S(1)} fusion(bf16[1024,896]{1,0:T(8,128)(2,1)S(1)} %copy-done, bf16[1024,1664]{0,1:T(8,128)(2,1)S(1)} %get-tuple-element.7, bf16[1024,1664]{0,1:T(8,128)(2,1)S(1)} %get-tuple-element.6), kind=kOutput, calls=%fused_computation.13 | convolution fusion | flops 6123520000 | bytes 14614528 | tf_op jit(solution)/shard_map/dot_general | solution.py:26
  743.8 2.1 fusion.16
  745.8 5.4 copy.10
  751.2 3.5 copy.11
Async XLA Ops:
  7.2 41.3 %all-gather.5.cloned.1.call-start = ((), (), s32[]{:S(2)}) async-start(), calls=%async_computation.1 | async-start | bytes 1949696 | tf_op jit(solution)/shard_map/all_gather | solution.py:21
  7.9 138.0 %all-gather.3.cloned.1.call-start = ((), (), s32[]{:S(2)}) async-start(), calls=%async_computation | async-start | bytes 3620864 | tf_op jit(solution)/shard_map/all_gather | solution.py:24
  8.6 717.5 %all-reduce.2.cloned.1.call-start = ((), (), s32[]{:S(2)}) async-start(), calls=%async_computation.2 | async-start | bytes 27262976 | tf_op jit(solution)/shard_map/psum | solution.py:23
  726.2 6.7 copy-start
Sparse Core Ops, SparseCore 0:
  9.8 38.6 all-gather.4
  51.1 94.8 all-gather.2
  148.6 577.5 all-reduce.1
where the time goes:
time: 767 us; the launch traced here: 761 us
  waiting for transfers between devices  701 us (91%)
  matrix products  24.4 us (3%)
  local copies, waits for them, and re-layouts  15.2 us (2%)
  between operations  13.8 us (2%)
    psum x1, waiting for transfers between devices, local(): preacts = lax.psum(partial_pre, 'row')  576 us
    all_gather x1, waiting for transfers between devices, local(): cotangent_all = lax.all_gather(upstream, 'row', axis=0, tiled=True)  83.9 us
    all_gather x1, waiting for transfers between devices, local(): gathered = lax.all_gather(tokens, 'col', axis=0, tiled=True)  39.8 us
  transfers between devices with their start and end apart: 3, of which 3 were waited for; matrix products, arithmetic and copies ran while one was open for 2% of the time, Pallas kernels for 0%

commit v1 on v0

v1 whole, which is shorter than its diff:
```python
import functools

import jax
import jax.numpy as jnp
from jax import lax
from jax.experimental import pallas as pl
from jax.experimental.pallas import tpu as pltpu
from jax.sharding import PartitionSpec as P

MESH = pl.DeviceIdType.MESH
F32 = jnp.float32
BF16 = jnp.bfloat16

NZ = 8
TB = 64
NT = 1024
DL = 896
FL = 1664
LANE = 128

ZT, YT = 6, 7
ZW, YW = ZT * LANE, YT * LANE
PHASES = ((3, 2), (2, 2), (2, 2))


def streams():
    out = []
    off, ycol, zcol = 0, 0, 0
    for ny, nz in PHASES:
        y = dict(kind="y", off=off, w=ny * LANE, col=ycol, gcol=ZW + ycol)
        off += 2 * ny * LANE
        ycol += ny * LANE
        zs = dict(kind="z", off=off, w=nz * LANE, col=zcol, gcol=zcol)
        off += 2 * nz * LANE
        zcol += nz * LANE
        out.append((y, zs))
    return out


def rcopy(src, dst, ssem, rsem, dev):
    return pltpu.make_async_remote_copy(
        src_ref=src, dst_ref=dst, send_sem=ssem, recv_sem=rsem, device_id=dev, device_id_type=MESH
    )


def kernel(
    x_ref, wg_ref, wu_ref, up_ref, gg_ref, gu_ref,
    xb, xt, wb, ub, zsz, zrz, zsy, zry, yown, ysend, yrecv, zfin, zfs, zfr, dall, gout,
    wsem, g_s, g_r, f_s, f_r, zz_s, zz_r, zy_s, zy_r, ye_s, ye_r, zf_s, zf_r,
    ay_s, ay_r, az_s, az_r, yf_s, yf_r, zx_s, zx_r, osem,
):
    row = lax.axis_index("row")
    col = lax.axis_index("col")
    z, h = lax.div(row, 2), lax.rem(row, 2)
    q, core = lax.div(col, 2), lax.rem(col, 2)
    zdev = ((lax.rem(z + 1, NZ) * 2 + h, col), (lax.rem(z + NZ - 1, NZ) * 2 + h, col))
    ydev = (z * 2 + 1 - h, col)
    cdev = (row, q * 2 + 1 - core)

    def qdev(i):
        return (row, lax.rem(q + i, NZ) * 2 + core)

    loads = [
        pltpu.make_async_copy(wg_ref.at[:, pl.ds(0, ZW)], wb.at[:, pl.ds(0, ZW)], wsem.at[0]),
        pltpu.make_async_copy(wu_ref.at[:, pl.ds(0, ZW)], wb.at[:, pl.ds(ZW, ZW)], wsem.at[1]),
        pltpu.make_async_copy(wg_ref.at[:, pl.ds(ZW, YW)], wb.at[:, pl.ds(2 * ZW, YW)], wsem.at[2]),
        pltpu.make_async_copy(wu_ref.at[:, pl.ds(ZW, YW)], wb.at[:, pl.ds(2 * ZW + YW, YW)], wsem.at[3]),
        pltpu.make_async_copy(up_ref, ub, wsem.at[4]),
    ]

    def xrows(c):
        return xb.at[pl.ds(pl.multiple_of(c * TB, TB), TB), :]

    own_x = pltpu.make_async_copy(x_ref, xrows(col), g_r.at[0])
    own_x.start()
    for c in loads:
        c.start()

    barrier = pltpu.get_barrier_semaphore()
    partners = [zdev[0], zdev[1], ydev, cdev] + [qdev(i) for i in range(1, NZ)]
    for dev in partners:
        pl.semaphore_signal(barrier, inc=1, device_id=dev, device_id_type=MESH)
    zrz[:, 0:2] = jnp.zeros((2, 2, 2 * TB, ZW), BF16)
    zry[:, 0:2] = jnp.zeros((2, 2, TB, YW), BF16)
    pl.semaphore_wait(barrier, len(partners))

    def gcopy(i):
        return rcopy(x_ref, xrows(col), g_s.at[i], g_r.at[i], qdev(i))

    for i in range(1, NZ):
        gcopy(i).start()

    def block_of(i):
        return lax.rem(q + NZ - i, NZ) * 2

    def fcopy(i):
        rows = xrows(block_of(i) + core)
        return rcopy(rows, rows, f_s.at[i], f_r.at[i], cdev)

    def fwait(i):
        rows = xrows(block_of(i) + 1 - core)
        return rcopy(rows, rows, f_s.at[i], f_r.at[i], cdev)

    for i in range(NZ):
        rows = xrows(block_of(i) + core)
        pltpu.make_async_copy(x_ref, rows, g_r.at[i]).wait()
        fcopy(i).start()
    for c in loads:
        c.wait()
    for i in range(NZ):
        fwait(i).wait_recv()

    def tokens_for(zz):
        a = pl.multiple_of(zz * 2 * TB + (1 - h) * TB, TB)
        b = pl.multiple_of(zz * 2 * TB + h * TB, TB)
        return jnp.concatenate([xb[pl.ds(a, TB), :], xb[pl.ds(b, TB), :]], axis=0)

    def zzcopy(d, t):
        return rcopy(zsz.at[d, t], zrz.at[d, t + 2], zz_s.at[d, t], zz_r.at[d, t], zdev[d])

    def zycopy(d, t):
        return rcopy(zsy.at[d, t], zry.at[d, t + 2], zy_s.at[d, t], zy_r.at[d, t], zdev[d])

    def yecopy(rel, half):
        return rcopy(ysend.at[rel, half], yrecv.at[rel, half], ye_s.at[rel, half], ye_r.at[rel, half], ydev)

    def zfcopy(half):
        return rcopy(zfs.at[half], zfr.at[half], zf_s.at[half], zf_r.at[half], ydev)

    def half_of(d, t):
        return lax.rem(t, 2) if d == 0 else 1 - lax.rem(t, 2)

    def rel_of(d, t):
        o = 4 - lax.rem(t, 2) - lax.div(t, 2)
        return o if d == 0 else NZ - o

    def z_step(t):
        for d in range(2):
            half = half_of(d, t)
            xd = tokens_for(lax.rem(z + rel_of(d, t), NZ))
            cols = pl.ds(pl.multiple_of(half * ZW, LANE), ZW)
            acc = jnp.dot(xd, wb[:, cols], preferred_element_type=F32)

            @pl.when(t >= 2)
            def _():
                zzcopy(d, t - 2).wait_recv()

            zsz[d, t] = (acc + zrz[d, t].astype(F32)).astype(BF16)
            zzcopy(d, t).start()

    def y_step(t):
        odd = lax.rem(t, 2)
        rel = (1 - odd) * (4 + lax.div(t, 2)) + odd * lax.div(7 - t, 2)
        zz = lax.rem(z + rel, NZ)
        xd = tokens_for(zz)
        for half in range(2):
            acc = jnp.dot(xd, wb[:, 2 * ZW + half * YW : 2 * ZW + (half + 1) * YW], preferred_element_type=F32)
            ysend[rel, half] = acc[:TB].astype(BF16)
            yecopy(rel, half).start()
            yown[rel, half] = acc[TB:]
        rows = pl.ds(pl.multiple_of(zz * 2 * TB, 2 * TB), 2 * TB)
        xt[:, rows] = xb[rows, :].T

    @pl.loop(0, NZ - 1)
    def _(t):
        z_step(t)
        y_step(t)

    y_step(jnp.int32(NZ - 1))

    def yz_step(t):
        for d in range(2):
            half = half_of(d, t)
            rel = rel_of(d, t)
            yecopy(rel, half).wait_recv()

            @pl.when(t >= 2)
            def _():
                zycopy(d, t - 2).wait_recv()

            acc = yown[rel, half] + yrecv[rel, half].astype(F32) + zry[d, t].astype(F32)
            zsy[d, t] = acc.astype(BF16)
            zycopy(d, t).start()

    @pl.loop(0, 3)
    def _(t):
        yz_step(t)

    for d in range(2):
        for t in (5, 6):
            zzcopy(d, t).wait_recv()
    xd = tokens_for(z)
    for half in range(2):
        acc = jnp.dot(xd, wb[:, half * ZW : (half + 1) * ZW], preferred_element_type=F32)
        acc = acc + zrz[0, 8 - half].astype(F32) + zrz[1, 7 + half].astype(F32)
        zfs[half] = acc[:TB].astype(BF16)
        zfcopy(half).start()
        zfin[half] = acc[TB:]

    @pl.loop(3, NZ - 1)
    def _(t):
        yz_step(t)

    my_rows = pl.ds(pl.multiple_of(row * TB, TB), TB)

    def store_grads(s, gate, up):
        w, off = s["w"], s["off"]
        u = ub[:, s["gcol"] : s["gcol"] + w].astype(F32)
        squash = jax.nn.sigmoid(gate)
        dall[my_rows, off : off + w] = (u * up * squash * (1.0 + gate * (1.0 - squash))).astype(BF16)
        dall[my_rows, off + w : off + 2 * w] = (u * gate * squash).astype(BF16)

    phases = streams()
    other_rows = pl.ds(pl.multiple_of((row + 1 - 2 * h) * TB, TB), TB)

    def zxcopy(p, rows):
        s = phases[p][1]
        ref = dall.at[rows, pl.ds(s["off"], 2 * s["w"])]
        return rcopy(ref, ref, zx_s.at[p], zx_r.at[p], ydev)

    def ag_slice(s, half, zz):
        cols = pl.ds(s["off"] + half * s["w"], s["w"])
        if s["kind"] == "y":
            return dall.at[pl.ds(pl.multiple_of(zz * 2 * TB + h * TB, TB), TB), cols]
        return dall.at[pl.ds(pl.multiple_of(zz * 2 * TB, 2 * TB), 2 * TB), cols]

    def agcopy(p, k, d, t, arriving=False):
        s = phases[p][k]
        half = t % 2 if d == 0 else 1 - t % 2
        hops = t // 2 + (1 if arriving else 0)
        zz = lax.rem(z + (NZ - hops if d == 0 else hops), NZ)
        ref = ag_slice(s, half, zz)
        ss, rs = ((ay_s, ay_r), (az_s, az_r))[k]
        return rcopy(ref, ref, ss.at[p, d, t], rs.at[p, d, t], zdev[d])

    def yfcopy(p, d, t, arriving=False):
        s = phases[p][0]
        if d == 2:
            half, zz, n = t, z, t
        else:
            half = t % 2 if d == 0 else 1 - t % 2
            hops = t // 2 + 1
            zz = lax.rem(z + (NZ - hops if d == 0 else hops), NZ)
            n = 2 + d * 7 + t
        hh = 1 - h if arriving else h
        ref = dall.at[
            pl.ds(pl.multiple_of(zz * 2 * TB + hh * TB, TB), TB), pl.ds(s["off"] + half * s["w"], s["w"])
        ]
        return rcopy(ref, ref, yf_s.at[p, n], yf_r.at[p, n], ydev)

    def out_copies(p, k):
        s = phases[p][k]
        off, w, g = s["off"], s["w"], s["gcol"]
        return [
            pltpu.make_async_copy(gout.at[:, pl.ds(off, w)], gg_ref.at[:, pl.ds(g, w)], osem.at[p, k, 0]),
            pltpu.make_async_copy(gout.at[:, pl.ds(off + w, w)], gu_ref.at[:, pl.ds(g, w)], osem.at[p, k, 1]),
        ]

    def weight_grads(p, k):
        s = phases[p][k]

        @pl.loop(0, 2 * s["w"] // 256)
        def _(n):
            cols = pl.ds(pl.multiple_of(s["off"] + n * 256, 256), 256)
            gout[:, cols] = jnp.dot(xt[...], dall[:, cols], preferred_element_type=F32).astype(BF16)

        for c in out_copies(p, k):
            c.start()

    def start_own(p, k):
        for t in range(2):
            for d in range(2):
                agcopy(p, k, d, t).start()
        if k == 0:
            for half in range(2):
                yfcopy(p, 2, half).start()

    def take(p, k, d, t):
        agcopy(p, k, d, t, arriving=True).wait_recv()
        if t < 5:
            agcopy(p, k, d, t + 2).start()
        if k == 0:
            yfcopy(p, d, t).start()

    def y_done(p):
        for half in range(2):
            yfcopy(p, 2, half, arriving=True).wait_recv()
        for t in range(7):
            for d in range(2):
                yfcopy(p, d, t, arriving=True).wait_recv()

    for half in range(2):
        zfcopy(half).wait_recv()
    for p, (_, s) in enumerate(phases):
        c = slice(s["col"], s["col"] + s["w"])
        store_grads(s, zfin[0, :, c] + zfr[0, :, c].astype(F32), zfin[1, :, c] + zfr[1, :, c].astype(F32))
        zxcopy(p, my_rows).start()

    for d in range(2):
        for t in (5, 6):
            zycopy(d, t).wait_recv()
    for half in range(2):
        yecopy(0, half).wait_recv()
    for p, (s, _) in enumerate(phases):
        c = slice(s["col"], s["col"] + s["w"])
        pre = [
            yown[0, a, :, c] + yrecv[0, a, :, c].astype(F32)
            + zry[0, 8 - a, :, c].astype(F32) + zry[1, 7 + a, :, c].astype(F32)
            for a in range(2)
        ]
        store_grads(s, pre[0], pre[1])
        if p == 0:
            start_own(0, 0)

    for p in range(len(phases)):
        if p == 0:
            zxcopy(0, other_rows).wait_recv()
            start_own(0, 1)
        for t in range(5):
            for k in range(2):
                for d in range(2):
                    take(p, k, d, t)
            if p and t == 1:
                weight_grads(p - 1, 1)
            if p and t == 3:
                y_done(p - 1)
                weight_grads(p - 1, 0)
        if p + 1 < len(phases):
            start_own(p + 1, 0)
            zxcopy(p + 1, other_rows).wait_recv()
            start_own(p + 1, 1)
        for t in (5, 6):
            for k in range(2):
                for d in range(2):
                    take(p, k, d, t)
    last = len(phases) - 1
    weight_grads(last, 1)
    y_done(last)
    weight_grads(last, 0)

    for i in range(1, NZ):
        gcopy(i).wait_send()
    for i in range(NZ):
        fcopy(i).wait_send()

    @pl.loop(0, 7)
    def _(t):
        for d in range(2):
            zzcopy(d, t).wait_send()
            zycopy(d, t).wait_send()

    @pl.loop(0, NZ)
    def _(rel):
        for half in range(2):
            yecopy(rel, half).wait_send()

    for half in range(2):
        zfcopy(half).wait_send()
    for p in range(len(phases)):
        zxcopy(p, my_rows).wait_send()
        for t in range(7):
            for d in range(2):
                for k in range(2):
                    agcopy(p, k, d, t).wait_send()
                yfcopy(p, d, t).wait_send()
        for half in range(2):
            yfcopy(p, 2, half).wait_send()
        for k in range(2):
            for c in out_copies(p, k):
                c.wait()


def local(tokens, gate_weight, up_weight, upstream):
    n = len(PHASES)
    dma = pltpu.SemaphoreType.DMA
    any_spec = pl.BlockSpec(memory_space=pl.ANY)
    return pl.pallas_call(
        kernel,
        out_shape=(jax.ShapeDtypeStruct((DL, FL), BF16), jax.ShapeDtypeStruct((DL, FL), BF16)),
        in_specs=[any_spec] * 4,
        out_specs=(any_spec, any_spec),
        scratch_shapes=[
            pltpu.VMEM((NT, DL), BF16),
            pltpu.VMEM((DL, NT), BF16),
            pltpu.VMEM((DL, 2 * FL), BF16),
            pltpu.VMEM((TB, FL), BF16),
            pltpu.VMEM((2, 7, 2 * TB, ZW), BF16),
            pltpu.VMEM((2, 9, 2 * TB, ZW), BF16),
            pltpu.VMEM((2, 7, TB, YW), BF16),
            pltpu.VMEM((2, 9, TB, YW), BF16),
            pltpu.VMEM((NZ, 2, TB, YW), F32),
            pltpu.VMEM((NZ, 2, TB, YW), BF16),
            pltpu.VMEM((NZ, 2, TB, YW), BF16),
            pltpu.VMEM((2, TB, ZW), F32),
            pltpu.VMEM((2, TB, ZW), BF16),
            pltpu.VMEM((2, TB, ZW), BF16),
            pltpu.VMEM((NT, 2 * FL), BF16),
            pltpu.VMEM((DL, 2 * FL), BF16),
            dma((5,)),
            dma((NZ,)), dma((NZ,)),
            dma((NZ,)), dma((NZ,)),
            dma((2, 7)), dma((2, 7)),
            dma((2, 7)), dma((2, 7)),
            dma((NZ, 2)), dma((NZ, 2)),
            dma((2,)), dma((2,)),
            dma((n, 2, 7)), dma((n, 2, 7)),
            dma((n, 2, 7)), dma((n, 2, 7)),
            dma((n, 16)), dma((n, 16)),
            dma((n,)), dma((n,)),
            dma((n, 2, 2)),
        ],
        compiler_params=pltpu.CompilerParams(
            collective_id=0, has_side_effects=True, vmem_limit_bytes=60 * 1024 * 1024
        ),
    )(tokens, gate_weight, up_weight, upstream)


def solution(mesh):
    return jax.shard_map(
        local,
        mesh=mesh,
        in_specs=(P("col", "row"), P("row", "col"), P("row", "col"), P("row", "col")),
        out_specs=(P("row", "col"), P("row", "col")),
        check_vma=False,
    )
```

time: 767 us -> 139 us (0.18)
  waiting for transfers between devices: 701 us -> 0 us
  Pallas kernels: 0 us -> 131 us
  matrix products: 24.4 us -> 0 us
  between operations: 13.8 us -> 0.65 us
  local copies, waits for them, and re-layouts: 15.2 us -> 5.43 us
    psum x1 -> x0, waiting for transfers between devices: 576 us -> none  [local(): preacts = lax.psum(partial_pre, 'row')]
    pallas_call x0 -> x1, Pallas kernels: none -> 131 us  [local(): pl.pallas_call(kernel, out_shape=(jax.ShapeDtypeStruct((DL, FL), BF16), j...]
    all_gather x2 -> x0, waiting for transfers between devices: 124 us -> none  [the longest x1 83.9 us: local(): cotangent_all = lax.all_gather(upstream, 'row', axis=0, tiled=True)]
    dot_general x2 -> x0, matrix products: 24.4 us -> none  [the longest x1 13.5 us: local(): partial_pre = jnp.dot(gathered, weights, preferred_element_type=jnp.float32)]
  transfers between devices with their start and end apart: 3 -> 0, of which waited for: 3 -> 0; matrix products, arithmetic and copies ran while one was open for 2% -> 0% of each run, Pallas kernels for 0% -> 0%
where the time goes in v1:
time: 139 us; the launch traced here: 137 us
  Pallas kernels  131 us (94%)
  local copies, waits for them, and re-layouts  5.43 us (4%)
    pallas_call x1, Pallas kernels, local(): pl.pallas_call(kernel, out_shape=(jax.ShapeDtypeStruct((DL, FL), BF16), j...  131 us
    unnamed x4, local copies, waits for them, and re-layouts  5.43 us

profile of v1, /device:TPU:2, one launch (start us, length us, event | category | flops | bytes accessed | tf_op | source)
XLA Modules:
  0.0 137.3 jit_solution(16021238457351027418)
XLA Ops:
  0.6 131.2 %shard_map.59 = (bf16[896,1664]{1,0:T(8,128)(2,1)}, bf16[896,1664]{1,0:T(8,128)(2,1)}) custom-call(bf16[64,896]{1,0:T(8,128)(2,1)} %x_ref.1, bf16[896,1664]{1,0:T(8,128)(2,1)} %wg_ref.1, bf16[896,1664]{1,0:T(8,128)(2,1)} %wu_ref.1, bf16[64,1664]{1,0:T(8,128)(2,1)} %up_ref.1), custom_call_target="tpu_custom_call" | custom-call | tf_op jit(solution)/shard_map/pallas_call | solution.py:377
  131.8 0.0 copy-start
  131.8 3.8 %copy.8 = bf16[896,1664]{1,0:T(8,128)(2,1)} copy(bf16[896,1664]{1,0:T(8,128)(2,1)} %get-tuple-element.4) | data formatting | bytes 5963776
  135.7 0.0 copy-done
  135.7 1.6 %copy.9 = bf16[896,1664]{1,0:T(8,128)(2,1)} copy(bf16[896,1664]{1,0:T(8,128)(2,1)S(1)} %copy-done) | data formatting | bytes 5963776
Async XLA Ops:
  131.8 3.8 %copy-start = (bf16[896,1664]{1,0:T(8,128)(2,1)S(1)}, bf16[896,1664]{1,0:T(8,128)(2,1)}, u32[]{:S(2)}) copy-start(bf16[896,1664]{1,0:T(8,128)(2,1)} %get-tuple-element.5) | copy-start | bytes 8945668

commit v2 on v1

--- a/solution.py
+++ b/solution.py
@@ -44,10 +44,10 @@
 
 
 def kernel(
-    x_ref, wg_ref, wu_ref, up_ref, gg_ref, gu_ref,
-    xb, xt, wb, ub, zsz, zrz, zsy, zry, yown, ysend, yrecv, zfin, zfs, zfr, dall, gout,
+    x_ref, wg_ref, wu_ref, up_ref, gout, xt, dall,
+    xb, wb, ub, zsz, zrz, zsy, zry, yown, ysend, yrecv, zfin, zfs, zfr,
     wsem, g_s, g_r, f_s, f_r, zz_s, zz_r, zy_s, zy_r, ye_s, ye_r, zf_s, zf_r,
-    ay_s, ay_r, az_s, az_r, yf_s, yf_r, zx_s, zx_r, osem,
+    ay_s, ay_r, az_s, az_r, yf_s, yf_r, zx_s, zx_r,
 ):
     row = lax.axis_index("row")
     col = lax.axis_index("col")
@@ -57,58 +57,91 @@
     ydev = (z * 2 + 1 - h, col)
     cdev = (row, q * 2 + 1 - core)
 
-    def qdev(i):
-        return (row, lax.rem(q + i, NZ) * 2 + core)
+    xx, yl = lax.div(q, 2), lax.rem(q, 2)
+    ql = q + 1 - 2 * yl
+    ldev = (row, ql * 2 + core)
+
+    def xdev(i):
+        return (row, (lax.rem(xx + i, 4) * 2 + yl) * 2 + core)
 
     loads = [
+        pltpu.make_async_copy(wg_ref.at[:, pl.ds(ZW, YW)], wb.at[:, pl.ds(2 * ZW, YW)], wsem.at[2]),
+        pltpu.make_async_copy(wu_ref.at[:, pl.ds(ZW, YW)], wb.at[:, pl.ds(2 * ZW + YW, YW)], wsem.at[3]),
         pltpu.make_async_copy(wg_ref.at[:, pl.ds(0, ZW)], wb.at[:, pl.ds(0, ZW)], wsem.at[0]),
         pltpu.make_async_copy(wu_ref.at[:, pl.ds(0, ZW)], wb.at[:, pl.ds(ZW, ZW)], wsem.at[1]),
-        pltpu.make_async_copy(wg_ref.at[:, pl.ds(ZW, YW)], wb.at[:, pl.ds(2 * ZW, YW)], wsem.at[2]),
-        pltpu.make_async_copy(wu_ref.at[:, pl.ds(ZW, YW)], wb.at[:, pl.ds(2 * ZW + YW, YW)], wsem.at[3]),
         pltpu.make_async_copy(up_ref, ub, wsem.at[4]),
     ]
 
     def xrows(c):
         return xb.at[pl.ds(pl.multiple_of(c * TB, TB), TB), :]
 
-    own_x = pltpu.make_async_copy(x_ref, xrows(col), g_r.at[0])
+    own_x = pltpu.make_async_copy(x_ref, xrows(col), g_r.at[q])
     own_x.start()
     for c in loads:
         c.start()
 
     barrier = pltpu.get_barrier_semaphore()
-    partners = [zdev[0], zdev[1], ydev, cdev] + [qdev(i) for i in range(1, NZ)]
+    partners = [zdev[0], zdev[1], ydev, cdev, ldev, xdev(1), xdev(2), xdev(3)]
     for dev in partners:
         pl.semaphore_signal(barrier, inc=1, device_id=dev, device_id_type=MESH)
     zrz[:, 0:2] = jnp.zeros((2, 2, 2 * TB, ZW), BF16)
     zry[:, 0:2] = jnp.zeros((2, 2, TB, YW), BF16)
     pl.semaphore_wait(barrier, len(partners))
 
-    def gcopy(i):
-        return rcopy(x_ref, xrows(col), g_s.at[i], g_r.at[i], qdev(i))
-
-    for i in range(1, NZ):
-        gcopy(i).start()
-
-    def block_of(i):
-        return lax.rem(q + NZ - i, NZ) * 2
-
-    def fcopy(i):
-        rows = xrows(block_of(i) + core)
-        return rcopy(rows, rows, f_s.at[i], f_r.at[i], cdev)
-
-    def fwait(i):
-        rows = xrows(block_of(i) + 1 - core)
-        return rcopy(rows, rows, f_s.at[i], f_r.at[i], cdev)
-
-    for i in range(NZ):
-        rows = xrows(block_of(i) + core)
-        pltpu.make_async_copy(x_ref, rows, g_r.at[i]).wait()
-        fcopy(i).start()
+    def own_copy(n, dev):
+        return rcopy(x_ref, xrows(col), g_s.at[n], g_r.at[q], dev)
+
+    def pass_copy(n, dev):
+        rows = xrows(ql * 2 + core)
+        return rcopy(rows, rows, g_s.at[n], g_r.at[ql], dev)
+
+    def fcopy(b):
+        rows = xrows(b * 2 + core)
+        return rcopy(rows, rows, f_s.at[b], f_r.at[b], cdev)
+
+    own_core = rcopy(x_ref, xrows(col), f_s.at[q], f_r.at[q], cdev)
+
+    def fwait(b):
+        rows = xrows(b * 2 + 1 - core)
+        rcopy(rows, rows, f_s.at[b], f_r.at[b], cdev).wait_recv()
+
+    def gwait(b):
+        pltpu.make_async_copy(x_ref, xrows(b * 2 + core), g_r.at[b]).wait()
+
+    def send_own():
+        for i in (2, 1, 3):
+            own_copy(i, xdev(i)).start()
+
+    def send_neighbour():
+        gwait(ql)
+        for i in (2, 1, 3):
+            pass_copy(3 + i, xdev(i)).start()
+        fcopy(ql).start()
+
+    own_copy(0, ldev).start()
+    own_core.start()
+    first = lax.rem(z + 4, NZ)
+
+    @pl.when(ql == first)
+    def _():
+        send_neighbour()
+
+    send_own()
+    gwait(q)
     for c in loads:
         c.wait()
-    for i in range(NZ):
-        fwait(i).wait_recv()
+    fwait(q)
+
+    def arrive(b):
+        @pl.when(jnp.logical_and(b != q, b != ql))
+        def _():
+            gwait(b)
+            fcopy(b).start()
+
+    def arrived(b):
+        @pl.when(b != q)
+        def _():
+            fwait(b)
 
     def tokens_for(zz):
         a = pl.multiple_of(zz * 2 * TB + (1 - h) * TB, TB)
@@ -148,9 +181,7 @@
             zsz[d, t] = (acc + zrz[d, t].astype(F32)).astype(BF16)
             zzcopy(d, t).start()
 
-    def y_step(t):
-        odd = lax.rem(t, 2)
-        rel = (1 - odd) * (4 + lax.div(t, 2)) + odd * lax.div(7 - t, 2)
+    def y_part(rel):
         zz = lax.rem(z + rel, NZ)
         xd = tokens_for(zz)
         for half in range(2):
@@ -161,7 +192,37 @@
         rows = pl.ds(pl.multiple_of(zz * 2 * TB, 2 * TB), 2 * TB)
         xt[:, rows] = xb[rows, :].T
 
-    @pl.loop(0, NZ - 1)
+    def rel_at(j):
+        odd = lax.rem(j, 2)
+        return (1 - odd) * (4 + lax.div(j, 2)) + odd * lax.div(7 - j, 2)
+
+    def y_step(j):
+        rel = rel_at(j)
+
+        @pl.when(rel != rel_q)
+        def _():
+            y_part(rel)
+
+    def block(j):
+        return lax.rem(z + rel_at(jnp.int32(j)), NZ)
+
+    rel_q = lax.rem(q + NZ - z, NZ)
+    y_part(rel_q)
+
+    @pl.when(ql != first)
+    def _():
+        send_neighbour()
+
+    arrive(block(0))
+    arrived(block(0))
+    z_step(jnp.int32(0))
+    for j in range(1, NZ):
+        arrive(block(j))
+    y_step(jnp.int32(0))
+    for j in range(1, NZ):
+        arrived(block(j))
+
+    @pl.loop(1, NZ - 1)
     def _(t):
         z_step(t)
         y_step(t)
@@ -248,14 +309,6 @@
         ]
         return rcopy(ref, ref, yf_s.at[p, n], yf_r.at[p, n], ydev)
 
-    def out_copies(p, k):
-        s = phases[p][k]
-        off, w, g = s["off"], s["w"], s["gcol"]
-        return [
-            pltpu.make_async_copy(gout.at[:, pl.ds(off, w)], gg_ref.at[:, pl.ds(g, w)], osem.at[p, k, 0]),
-            pltpu.make_async_copy(gout.at[:, pl.ds(off + w, w)], gu_ref.at[:, pl.ds(g, w)], osem.at[p, k, 1]),
-        ]
-
     def weight_grads(p, k):
         s = phases[p][k]
 
@@ -264,8 +317,6 @@
             cols = pl.ds(pl.multiple_of(s["off"] + n * 256, 256), 256)
             gout[:, cols] = jnp.dot(xt[...], dall[:, cols], preferred_element_type=F32).astype(BF16)
 
-        for c in out_copies(p, k):
-            c.start()
 
     def start_own(p, k):
         for t in range(2):
@@ -334,14 +385,14 @@
                 for d in range(2):
                     take(p, k, d, t)
     last = len(phases) - 1
-    weight_grads(last, 1)
     y_done(last)
-    weight_grads(last, 0)
-
-    for i in range(1, NZ):
-        gcopy(i).wait_send()
+
+    own_copy(0, ldev).wait_send()
+    for i in (2, 1, 3):
+        own_copy(i, xdev(i)).wait_send()
+        pass_copy(3 + i, xdev(i)).wait_send()
     for i in range(NZ):
-        fcopy(i).wait_send()
+        fcopy(jnp.int32(i)).wait_send()
 
     @pl.loop(0, 7)
     def _(t):
@@ -365,23 +416,51 @@
                 yfcopy(p, d, t).wait_send()
         for half in range(2):
             yfcopy(p, 2, half).wait_send()
+
+
+def finish(gout, xt, dall, gg_ref, gu_ref, late, osem):
+    phases = streams()
+    last = len(phases) - 1
+    base = phases[last][0]["off"]
+    copies = []
+
+    def send(p, k, src, off):
+        s = phases[p][k]
+        w, g = s["w"], s["gcol"]
+        for a, ref in enumerate((gg_ref, gu_ref)):
+            c = pltpu.make_async_copy(src.at[:, pl.ds(off + a * w, w)], ref.at[:, pl.ds(g, w)], osem.at[p, k, a])
+            c.start()
+            copies.append(c)
+
+    for p in range(last):
         for k in range(2):
-            for c in out_copies(p, k):
-                c.wait()
+            send(p, k, gout, phases[p][k]["off"])
+    for k in range(2):
+        s = phases[last][k]
+
+        @pl.loop(0, 2 * s["w"] // 256)
+        def _(n):
+            src = pl.ds(pl.multiple_of(s["off"] + n * 256, 256), 256)
+            dst = pl.ds(pl.multiple_of(s["off"] - base + n * 256, 256), 256)
+            late[:, dst] = jnp.dot(xt[...], dall[:, src], preferred_element_type=F32).astype(BF16)
+
+        send(last, k, late, s["off"] - base)
+    for c in copies:
+        c.wait()
 
 
 def local(tokens, gate_weight, up_weight, upstream):
     n = len(PHASES)
     dma = pltpu.SemaphoreType.DMA
     any_spec = pl.BlockSpec(memory_space=pl.ANY)
-    return pl.pallas_call(
+    vmem_spec = pl.BlockSpec(memory_space=pltpu.VMEM)
+    gout, xt, dall = pl.pallas_call(
         kernel,
-        out_shape=(jax.ShapeDtypeStruct((DL, FL), BF16), jax.ShapeDtypeStruct((DL, FL), BF16)),
+        out_shape=(pltpu.VMEM((DL, 2 * FL), BF16), pltpu.VMEM((DL, NT), BF16), pltpu.VMEM((NT, 2 * FL), BF16)),
         in_specs=[any_spec] * 4,
-        out_specs=(any_spec, any_spec),
+        out_specs=(vmem_spec,) * 3,
         scratch_shapes=[
             pltpu.VMEM((NT, DL), BF16),
-            pltpu.VMEM((DL, NT), BF16),
             pltpu.VMEM((DL, 2 * FL), BF16),
             pltpu.VMEM((TB, FL), BF16),
             pltpu.VMEM((2, 7, 2 * TB, ZW), BF16),
@@ -394,8 +473,6 @@
             pltpu.VMEM((2, TB, ZW), F32),
             pltpu.VMEM((2, TB, ZW), BF16),
             pltpu.VMEM((2, TB, ZW), BF16),
-            pltpu.VMEM((NT, 2 * FL), BF16),
-            pltpu.VMEM((DL, 2 * FL), BF16),
             dma((5,)),
             dma((NZ,)), dma((NZ,)),
             dma((NZ,)), dma((NZ,)),
@@ -407,12 +484,20 @@
             dma((n, 2, 7)), dma((n, 2, 7)),
             dma((n, 16)), dma((n, 16)),
             dma((n,)), dma((n,)),
-            dma((n, 2, 2)),
         ],
         compiler_params=pltpu.CompilerParams(
-            collective_id=0, has_side_effects=True, vmem_limit_bytes=60 * 1024 * 1024
+            collective_id=0, has_side_effects=True, vmem_limit_bytes=44 * 1024 * 1024
         ),
     )(tokens, gate_weight, up_weight, upstream)
+    width = sum(2 * s["w"] for s in streams()[-1])
+    return pl.pallas_call(
+        finish,
+        out_shape=(jax.ShapeDtypeStruct((DL, FL), BF16), jax.ShapeDtypeStruct((DL, FL), BF16)),
+        in_specs=[vmem_spec] * 3,
+        out_specs=(any_spec, any_spec),
+        scratch_shapes=[pltpu.VMEM((DL, width), BF16), dma((n, 2, 2))],
+        compiler_params=pltpu.CompilerParams(vmem_limit_bytes=4 * 1024 * 1024),
+    )(gout, xt, dall)
 
 
 def solution(mesh):

time: 139 us -> 133 us (0.957); the launches traced: 137 us -> 133 us
  local copies, waits for them, and re-layouts: 5.43 us -> 0 us
    unnamed x4 -> x0, local copies, waits for them, and re-layouts: 5.43 us -> none
    pallas_call x1 -> x2, Pallas kernels: 131 us -> 132 us  [the longest x1 129 us: local(): pl.pallas_call(kernel, out_shape=(pltpu.VMEM((DL, 2 * FL), BF16), pltpu.V...]
where the time goes in v2:
time: 133 us
  Pallas kernels  132 us (99%)
    pallas_call x1, Pallas kernels, local(): pl.pallas_call(kernel, out_shape=(pltpu.VMEM((DL, 2 * FL), BF16), pltpu.V...  129 us
    pallas_call x1, Pallas kernels, local(): pl.pallas_call(finish, out_shape=(jax.ShapeDtypeStruct((DL, FL), BF16), j...  3.66 us

profile of v2, /device:TPU:2, one launch (start us, length us, event | category | flops | bytes accessed | tf_op | source)
XLA Modules:
  0.0 132.8 jit_solution(2880300424111869588)
XLA Ops:
  0.6 128.5 %shard_map.59 = (bf16[896,3328]{1,0:T(8,128)(2,1)S(1)}, bf16[896,1024]{1,0:T(8,128)(2,1)S(1)}, bf16[1024,3328]{1,0:T(8,128)(2,1)S(1)}) custom-call(bf16[64,896]{1,0:T(8,128)(2,1)} %x_ref.1, bf16[896,1664]{1,0:T(8,128)(2,1)} %wg_ref.1, bf16[896,1664]{1,0:T(8,128)(2,1)} %wu_ref.1, bf16[64,1664]{1,0:T(8,128)(2,1)} %up_ref.1), custom_call_target="tpu_custom_call" | custom-call | tf_op jit(solution)/shard_map/pallas_call | solution.py:457
  129.1 3.7 %shard_map.60 = (bf16[896,1664]{1,0:T(8,128)(2,1)}, bf16[896,1664]{1,0:T(8,128)(2,1)}) custom-call(bf16[896,3328]{1,0:T(8,128)(2,1)S(1)} %get-tuple-element.5.gout, bf16[896,1024]{1,0:T(8,128)(2,1)S(1)} %get-tuple-element.6.xt, bf16[1024,3328]{1,0:T(8,128)(2,1)S(1)} %get-tuple-element.7.dall), custom_call_target="tpu_custom_call" | custom-call | tf_op jit(solution)/shard_map/pallas_call | solution.py:493

commit v3 on v2

--- a/solution.py
+++ b/solution.py
@@ -18,21 +18,21 @@
 FL = 1664
 LANE = 128
 
-ZT, YT = 6, 7
+ZT, YT = 5, 8
 ZW, YW = ZT * LANE, YT * LANE
-PHASES = ((3, 2), (2, 2), (2, 2))
+PHASES = ((5, 3), (2, 3))
 
 
 def streams():
     out = []
-    off, ycol, zcol = 0, 0, 0
+    off, zt, yt = 0, 0, sum(nz for _, nz in PHASES)
     for ny, nz in PHASES:
-        y = dict(kind="y", off=off, w=ny * LANE, col=ycol, gcol=ZW + ycol)
+        y = dict(kind="y", off=off, w=ny * LANE, gcol=yt * LANE)
         off += 2 * ny * LANE
-        ycol += ny * LANE
-        zs = dict(kind="z", off=off, w=nz * LANE, col=zcol, gcol=zcol)
+        yt += ny
+        zs = dict(kind="z", off=off, w=nz * LANE, gcol=zt * LANE)
         off += 2 * nz * LANE
-        zcol += nz * LANE
+        zt += nz
         out.append((y, zs))
     return out
 
@@ -263,15 +263,32 @@
         yz_step(t)
 
     my_rows = pl.ds(pl.multiple_of(row * TB, TB), TB)
-
-    def store_grads(s, gate, up):
-        w, off = s["w"], s["off"]
-        u = ub[:, s["gcol"] : s["gcol"] + w].astype(F32)
-        squash = jax.nn.sigmoid(gate)
-        dall[my_rows, off : off + w] = (u * up * squash * (1.0 + gate * (1.0 - squash))).astype(BF16)
-        dall[my_rows, off + w : off + 2 * w] = (u * gate * squash).astype(BF16)
-
     phases = streams()
+
+    def store_grads(lo, hi, pre):
+        for s in (s for phase in phases for s in phase):
+            a, b = max(lo, s["gcol"]), min(hi, s["gcol"] + s["w"])
+            if a >= b:
+                continue
+            gate, up = pre(0, a - lo, b - lo), pre(1, a - lo, b - lo)
+            off = s["off"] + a - s["gcol"]
+            u = ub[:, a:b].astype(F32)
+            squash = jax.nn.sigmoid(gate)
+            dall[my_rows, off : off + b - a] = (
+                u * up * squash * (1.0 + gate * (1.0 - squash))
+            ).astype(BF16)
+            off += s["w"]
+            dall[my_rows, off : off + b - a] = (u * gate * squash).astype(BF16)
+
+    def z_pre(half, a, b):
+        return zfin[half, :, a:b] + zfr[half, :, a:b].astype(F32)
+
+    def y_pre(half, a, b):
+        return (
+            yown[0, half, :, a:b] + yrecv[0, half, :, a:b].astype(F32)
+            + zry[0, 8 - half, :, a:b].astype(F32) + zry[1, 7 + half, :, a:b].astype(F32)
+        )
+
     other_rows = pl.ds(pl.multiple_of((row + 1 - 2 * h) * TB, TB), TB)
 
     def zxcopy(p, rows):
@@ -342,26 +359,21 @@
 
     for half in range(2):
         zfcopy(half).wait_recv()
+    store_grads(0, ZW, z_pre)
     for p, (_, s) in enumerate(phases):
-        c = slice(s["col"], s["col"] + s["w"])
-        store_grads(s, zfin[0, :, c] + zfr[0, :, c].astype(F32), zfin[1, :, c] + zfr[1, :, c].astype(F32))
-        zxcopy(p, my_rows).start()
+        if s["gcol"] + s["w"] <= ZW:
+            zxcopy(p, my_rows).start()
 
     for d in range(2):
         for t in (5, 6):
             zycopy(d, t).wait_recv()
     for half in range(2):
         yecopy(0, half).wait_recv()
-    for p, (s, _) in enumerate(phases):
-        c = slice(s["col"], s["col"] + s["w"])
-        pre = [
-            yown[0, a, :, c] + yrecv[0, a, :, c].astype(F32)
-            + zry[0, 8 - a, :, c].astype(F32) + zry[1, 7 + a, :, c].astype(F32)
-            for a in range(2)
-        ]
-        store_grads(s, pre[0], pre[1])
-        if p == 0:
-            start_own(0, 0)
+    store_grads(ZW, FL, y_pre)
+    start_own(0, 0)
+    for p, (_, s) in enumerate(phases):
+        if s["gcol"] + s["w"] > ZW:
+            zxcopy(p, my_rows).start()
 
     for p in range(len(phases)):
         if p == 0:
@@ -385,6 +397,7 @@
                 for d in range(2):
                     take(p, k, d, t)
     last = len(phases) - 1
+    weight_grads(last, 1)
     y_done(last)
 
     own_copy(0, ldev).wait_send()
@@ -432,19 +445,18 @@
             c.start()
             copies.append(c)
 
-    for p in range(last):
-        for k in range(2):
-            send(p, k, gout, phases[p][k]["off"])
-    for k in range(2):
-        s = phases[last][k]
-
-        @pl.loop(0, 2 * s["w"] // 256)
-        def _(n):
-            src = pl.ds(pl.multiple_of(s["off"] + n * 256, 256), 256)
-            dst = pl.ds(pl.multiple_of(s["off"] - base + n * 256, 256), 256)
-            late[:, dst] = jnp.dot(xt[...], dall[:, src], preferred_element_type=F32).astype(BF16)
-
-        send(last, k, late, s["off"] - base)
+    for p in range(last + 1):
+        for k in range(2 if p < last else 1):
+            send(p, 1 - k, gout, phases[p][1 - k]["off"])
+    s = phases[last][0]
+
+    @pl.loop(0, 2 * s["w"] // 256)
+    def _(n):
+        src = pl.ds(pl.multiple_of(base + n * 256, 256), 256)
+        dst = pl.ds(pl.multiple_of(n * 256, 256), 256)
+        late[:, dst] = jnp.dot(xt[...], dall[:, src], preferred_element_type=F32).astype(BF16)
+
+    send(last, 0, late, 0)
     for c in copies:
         c.wait()
 
@@ -489,7 +501,7 @@
             collective_id=0, has_side_effects=True, vmem_limit_bytes=44 * 1024 * 1024
         ),
     )(tokens, gate_weight, up_weight, upstream)
-    width = sum(2 * s["w"] for s in streams()[-1])
+    width = 2 * streams()[-1][0]["w"]
     return pl.pallas_call(
         finish,
         out_shape=(jax.ShapeDtypeStruct((DL, FL), BF16), jax.ShapeDtypeStruct((DL, FL), BF16)),

time: 133 us -> 128 us (0.962)
  Pallas kernels: 132 us -> 127 us
    pallas_call x1, Pallas kernels: 129 us -> 125 us  [local(): pl.pallas_call(kernel, out_shape=(pltpu.VMEM((DL, 2 * FL), BF16), pltpu.V...]
where the time goes in v3:
time: 128 us
  Pallas kernels  127 us (99%)
    pallas_call x1, Pallas kernels, local(): pl.pallas_call(kernel, out_shape=(pltpu.VMEM((DL, 2 * FL), BF16), pltpu.V...  125 us
    pallas_call x1, Pallas kernels, local(): pl.pallas_call(finish, out_shape=(jax.ShapeDtypeStruct((DL, FL), BF16), j...  2.62 us

profile of v3, /device:TPU:2, one launch (start us, length us, event | category | flops | bytes accessed | tf_op | source)
XLA Modules:
  0.0 128.0 jit_solution(16482400429136866496)
XLA Ops:
  0.6 124.7 %shard_map.59 = (bf16[896,3328]{1,0:T(8,128)(2,1)S(1)}, bf16[896,1024]{1,0:T(8,128)(2,1)S(1)}, bf16[1024,3328]{1,0:T(8,128)(2,1)S(1)}) custom-call(bf16[64,896]{1,0:T(8,128)(2,1)} %x_ref.1, bf16[896,1664]{1,0:T(8,128)(2,1)} %wg_ref.1, bf16[896,1664]{1,0:T(8,128)(2,1)} %wu_ref.1, bf16[64,1664]{1,0:T(8,128)(2,1)} %up_ref.1), custom_call_target="tpu_custom_call" | custom-call | tf_op jit(solution)/shard_map/pallas_call | solution.py:469
  125.4 2.6 %shard_map.60 = (bf16[896,1664]{1,0:T(8,128)(2,1)}, bf16[896,1664]{1,0:T(8,128)(2,1)}) custom-call(bf16[896,3328]{1,0:T(8,128)(2,1)S(1)} %get-tuple-element.5.gout, bf16[896,1024]{1,0:T(8,128)(2,1)S(1)} %get-tuple-element.6.xt, bf16[1024,3328]{1,0:T(8,128)(2,1)S(1)} %get-tuple-element.7.dall), custom_call_target="tpu_custom_call" | custom-call | tf_op jit(solution)/shard_map/pallas_call | solution.py:505

commit v4 on v3

--- a/solution.py
+++ b/solution.py
@@ -21,6 +21,7 @@
 ZT, YT = 5, 8
 ZW, YW = ZT * LANE, YT * LANE
 PHASES = ((5, 3), (2, 3))
+SPREAD = (((1, 0, 1),), ((1, 1, 3),), ((0, 0, 2),), ((0, 2, 4),), ((0, 4, 5),))
 
 
 def streams():
@@ -139,7 +140,7 @@
             fcopy(b).start()
 
     def arrived(b):
-        @pl.when(b != q)
+        @pl.when(jnp.logical_and(b != q, b != ql))
         def _():
             fwait(b)
 
@@ -199,7 +200,7 @@
     def y_step(j):
         rel = rel_at(j)
 
-        @pl.when(rel != rel_q)
+        @pl.when(jnp.logical_and(rel != rel_q, rel != rel_ql))
         def _():
             y_part(rel)
 
@@ -207,11 +208,15 @@
         return lax.rem(z + rel_at(jnp.int32(j)), NZ)
 
     rel_q = lax.rem(q + NZ - z, NZ)
+    rel_ql = lax.rem(ql + NZ - z, NZ)
     y_part(rel_q)
 
     @pl.when(ql != first)
     def _():
         send_neighbour()
+
+    fwait(ql)
+    y_part(rel_ql)
 
     arrive(block(0))
     arrived(block(0))
@@ -326,10 +331,10 @@
         ]
         return rcopy(ref, ref, yf_s.at[p, n], yf_r.at[p, n], ydev)
 
-    def weight_grads(p, k):
+    def weight_grads(p, k, lo=0, hi=None):
         s = phases[p][k]
 
-        @pl.loop(0, 2 * s["w"] // 256)
+        @pl.loop(lo, 2 * s["w"] // 256 if hi is None else hi)
         def _(n):
             cols = pl.ds(pl.multiple_of(s["off"] + n * 256, 256), 256)
             gout[:, cols] = jnp.dot(xt[...], dall[:, cols], preferred_element_type=F32).astype(BF16)
@@ -383,11 +388,11 @@
             for k in range(2):
                 for d in range(2):
                     take(p, k, d, t)
-            if p and t == 1:
-                weight_grads(p - 1, 1)
-            if p and t == 3:
-                y_done(p - 1)
-                weight_grads(p - 1, 0)
+            if p:
+                for k, lo, hi in SPREAD[t]:
+                    if k == 0 and lo == 0:
+                        y_done(p - 1)
+                    weight_grads(p - 1, k, lo, hi)
         if p + 1 < len(phases):
             start_own(p + 1, 0)
             zxcopy(p + 1, other_rows).wait_recv()

time: 128 us -> 127 us (level)
    pallas_call x1, Pallas kernels: 125 us -> 123 us  [local(): pl.pallas_call(kernel, out_shape=(pltpu.VMEM((DL, 2 * FL), BF16), pltpu.V...]
where the time goes in v4:
time: 127 us
  Pallas kernels  126 us (99%)
    pallas_call x1, Pallas kernels, local(): pl.pallas_call(kernel, out_shape=(pltpu.VMEM((DL, 2 * FL), BF16), pltpu.V...  123 us
    pallas_call x1, Pallas kernels, local(): pl.pallas_call(finish, out_shape=(jax.ShapeDtypeStruct((DL, FL), BF16), j...  2.62 us

profile of v4, /device:TPU:2, one launch (start us, length us, event | category | flops | bytes accessed | tf_op | source)
XLA Modules:
  0.0 126.6 jit_solution(15769943681946762878)
XLA Ops:
  0.6 123.3 %shard_map.59 = (bf16[896,3328]{1,0:T(8,128)(2,1)S(1)}, bf16[896,1024]{1,0:T(8,128)(2,1)S(1)}, bf16[1024,3328]{1,0:T(8,128)(2,1)S(1)}) custom-call(bf16[64,896]{1,0:T(8,128)(2,1)} %x_ref.1, bf16[896,1664]{1,0:T(8,128)(2,1)} %wg_ref.1, bf16[896,1664]{1,0:T(8,128)(2,1)} %wu_ref.1, bf16[64,1664]{1,0:T(8,128)(2,1)} %up_ref.1), custom_call_target="tpu_custom_call" | custom-call | tf_op jit(solution)/shard_map/pallas_call | solution.py:474
  123.9 2.6 %shard_map.60 = (bf16[896,1664]{1,0:T(8,128)(2,1)}, bf16[896,1664]{1,0:T(8,128)(2,1)}) custom-call(bf16[896,3328]{1,0:T(8,128)(2,1)S(1)} %get-tuple-element.5.gout, bf16[896,1024]{1,0:T(8,128)(2,1)S(1)} %get-tuple-element.6.xt, bf16[1024,3328]{1,0:T(8,128)(2,1)S(1)} %get-tuple-element.7.dall), custom_call_target="tpu_custom_call" | custom-call | tf_op jit(solution)/shard_map/pallas_call | solution.py:510
